TPU v7x, 32 devices: a whole 2x2x4 slice. The times are simulated.
32 devices in a mesh: fam: 4 (over z), ctx: 8 (over y, x, core).
Axes of the slice: x: 2, y: 2, z: 4, core: 2. Of those that a mesh axis runs over, the one named last changes fastest.
Arguments:
- queries: bfloat16 [4, 4096, 1024], P('fam', 'ctx'), may hold values from -7 to 7
- key_rows: bfloat16 [4, 4096, 1024], P('fam', 'ctx'), may hold values from -4 to 4
- value_rows: bfloat16 [4, 4096, 1024], P('fam', 'ctx'), may hold values from -6 to 6
- cotangent: bfloat16 [4, 4096, 1024], P('fam', 'ctx'), may hold values from -6 to 6
- out_weight: bfloat16 [1024, 1024], replicated, may hold values from -0.1875 to 0.1875
- prot_blocks: int32 [4, 8], P('fam'), may hold values from 1 to 8, 32 in all within a row
- last_fill: int32 [4, 8], P('fam'), may hold values from 1 to 128
- memory_slots: int32 [4, 128], P('fam'), may hold values from 0 to 511
Outputs:
- query_grad: bfloat16 [4, 4096, 1024], P('fam', 'ctx')
- key_grad: bfloat16 [4, 4096, 1024], P('fam', 'ctx')
- value_grad: bfloat16 [4, 4096, 1024], P('fam', 'ctx')
- weight_grad: float32 [1024, 1024], replicated
Inputs may be any that keep to these rules, and one draw needn't show every extreme that they name: `prot_blocks`: each family's protein lengths, in blocks, sum to 32, and the longest has exactly 8 blocks.
All inputs are finite; a program needn't handle non-finite values.
Results may differ from a plain program's by a relative error of at most 0.015.
Values may be sent and summed in bfloat16 or wider, within the bound.
No kernel may reach another device: no remote copies, remote signals or barrier semaphores. Data moves between devices by JAX's collectives and lax.ppermute only.
A program may use at most 128 MiB of HBM per device.

v0:
```python
import jax
import jax.numpy as jnp
from jax import lax
from jax.sharding import PartitionSpec as P

HEAD_DIM = 64
W = 512
BLK = 128


NEG_FILL = -1e30


def passed_along(value, axis, steps):
    count = lax.axis_size(axis)
    initial, last = (max(0, -steps), min(count, count - steps))
    return lax.ppermute(value, axis, [(source, source + steps) for source in range(initial, last)])


def protein_tables(prot_blocks, last_fill):
    prot_ends = jnp.cumsum(prot_blocks)
    starts = prot_ends - prot_blocks
    valid_len = (prot_blocks - 1) * BLK + last_fill
    return (prot_ends, starts, valid_len)


def token_info(positions, tables):
    prot_ends, starts, valid_len = tables
    prot_count = prot_ends.shape[0]
    block_ids = jnp.floor_divide(positions, BLK)
    protein = jnp.sum((block_ids[:, None] >= prot_ends[None, :]).astype(jnp.int32), axis=1)
    onehot = protein[:, None] == jnp.arange(prot_count, dtype=jnp.int32)[None, :]
    first_block = jnp.sum(jnp.where(onehot, starts[None, :], 0), axis=1)
    allowed = jnp.sum(jnp.where(onehot, valid_len[None, :], 0), axis=1)
    is_valid = (positions >= 0) & (protein < prot_count) & (positions - first_block * BLK < allowed)
    return (protein, is_valid)


def band_mask(query_pos, query_info, key_pos, key_info):
    return (
        query_info[1][:, None]
        & key_info[1][None, :]
        & (query_info[0][:, None] == key_info[0][None, :])
        & (key_pos[None, :] <= query_pos[:, None])
        & (query_pos[:, None] - key_pos[None, :] < W)
    )


def columns_of(array, column, span):
    return lax.dynamic_slice_in_dim(array, column, span, 1)


def add_into(target, update, row_start, column):
    row_index = jnp.asarray(row_start, jnp.int32)
    current = lax.dynamic_slice(target, (row_index, column), update.shape)
    return lax.dynamic_update_slice(target, current + update, (row_index, column))


def attend(query_blk, grad_blk, key_blk, value_blk, live_mask):
    scale = HEAD_DIM ** (-0.5)
    scores = (
        jnp.einsum("qge,kge->gqk", query_blk, key_blk, preferred_element_type=jnp.float32) * scale
    )
    live = live_mask[None]
    shifted = jnp.where(live, scores, NEG_FILL)
    row_max = jnp.max(shifted, axis=-1, keepdims=True)
    expo = jnp.where(live, jnp.exp(shifted - row_max), 0.0)
    row_sum = jnp.maximum(jnp.sum(expo, axis=-1, keepdims=True), 1.0)
    attn_prob = expo / row_sum
    prob_half = attn_prob.astype(jnp.bfloat16)
    attended = jnp.einsum(
        "gqk,kge->qge", prob_half, value_blk, preferred_element_type=jnp.float32
    ).astype(jnp.bfloat16)
    grad_prob = jnp.einsum("qge,kge->gqk", grad_blk, value_blk, preferred_element_type=jnp.float32)
    row_dot = jnp.sum(attn_prob * grad_prob, axis=-1, keepdims=True)
    grad_score = (attn_prob * (grad_prob - row_dot) * scale).astype(jnp.bfloat16)
    grad_query = jnp.einsum("gqk,kge->qge", grad_score, key_blk, preferred_element_type=jnp.float32)
    grad_key = jnp.einsum("gqk,qge->kge", grad_score, query_blk, preferred_element_type=jnp.float32)
    grad_value = jnp.einsum("gqk,qge->kge", prob_half, grad_blk, preferred_element_type=jnp.float32)
    return (attended, grad_query, grad_key, grad_value, row_max, row_sum, row_dot)


def per_device(
    queries, key_rows, value_rows, cotangent, out_weight, prot_blocks, last_fill, memory_slots
):
    query_loc = queries[0]
    key_loc = key_rows[0]
    value_loc = value_rows[0]
    grad_out = cotangent[0]
    tables = protein_tables(prot_blocks[0], last_fill[0])
    slots = memory_slots[0]
    tokens, width = query_loc.shape
    span = 2 * HEAD_DIM
    pair_count = width // span
    heads_total = width // HEAD_DIM
    ctx_size = lax.axis_size("ctx")
    ctx_index = lax.axis_index("ctx")
    slot_total = slots.shape[0]
    slot_dev = slot_total // ctx_size
    base = ctx_index * tokens
    positions = base + jnp.arange(tokens, dtype=jnp.int32)
    own_info = token_info(positions, tables)
    ext_pos = base - W + jnp.arange(W + tokens, dtype=jnp.int32)
    ext_info = token_info(ext_pos, tables)
    source = jnp.arange(slot_total, dtype=jnp.int32) // slot_dev * tokens + slots
    mem_info = token_info(source, tables)
    own_slots = lax.dynamic_slice_in_dim(slots, ctx_index * slot_dev, slot_dev)
    mem_keys, mem_values = (
        lax.all_gather(key_loc[own_slots], "ctx", axis=0, tiled=True),
        lax.all_gather(value_loc[own_slots], "ctx", axis=0, tiled=True),
    )
    halo_keys, halo_values = passed_along((key_loc, value_loc), "ctx", 1)
    ext_keys = jnp.concatenate([halo_keys, key_loc], axis=0)
    ext_values = jnp.concatenate([halo_values, value_loc], axis=0)
    grad_attn = jnp.einsum(
        "te,de->td", grad_out, out_weight, preferred_element_type=jnp.float32
    ).astype(jnp.bfloat16)
    masks = []
    query_info = (own_info[0], own_info[1])
    key_info = (ext_info[0], ext_info[1])
    band = band_mask(positions, query_info, ext_pos, key_info)
    memory = (
        query_info[1][:, None]
        & mem_info[1][None, :]
        & (mem_info[0][None, :] < query_info[0][:, None])
    )
    masks.append(jnp.concatenate([band, memory], axis=1))

    def pair_step(head_pair, carry):
        (
            query_grad,
            band_kgrad,
            band_vgrad,
            mem_kgrad,
            mem_vgrad,
            attn_rows,
            stat_max,
            stat_sum,
            stat_dot,
        ) = carry
        column = head_pair * span
        query_pair = columns_of(query_loc, column, span).reshape(tokens, 2, HEAD_DIM)
        dout_pair = columns_of(grad_attn, column, span).reshape(tokens, 2, HEAD_DIM)
        key_band = columns_of(ext_keys, column, span).reshape(W + tokens, 2, HEAD_DIM)
        value_band = columns_of(ext_values, column, span).reshape(W + tokens, 2, HEAD_DIM)
        key_memory = columns_of(mem_keys, column, span).reshape(slot_total, 2, HEAD_DIM)
        value_memory = columns_of(mem_values, column, span).reshape(slot_total, 2, HEAD_DIM)
        key_blk = jnp.concatenate([key_band, key_memory], axis=0)
        value_blk = jnp.concatenate([value_band, value_memory], axis=0)
        attended, grad_query, grad_key, grad_value, row_max, row_sum, row_dot = attend(
            query_pair, dout_pair, key_blk, value_blk, masks[0]
        )
        row_index = jnp.asarray(0, jnp.int32)
        query_grad = lax.dynamic_update_slice(
            query_grad, grad_query.reshape(W, span), (row_index, column)
        )
        attn_rows = lax.dynamic_update_slice(
            attn_rows, attended.reshape(W, span), (row_index, column)
        )
        band_kgrad = add_into(band_kgrad, grad_key[: 2 * W].reshape(2 * W, span), 0, column)
        band_vgrad = add_into(band_vgrad, grad_value[: 2 * W].reshape(2 * W, span), 0, column)
        mem_kgrad = add_into(mem_kgrad, grad_key[2 * W :].reshape(slot_total, span), 0, column)
        mem_vgrad = add_into(mem_vgrad, grad_value[2 * W :].reshape(slot_total, span), 0, column)
        stat_col = head_pair * 2
        zero_row = jnp.asarray(0, jnp.int32)
        stat_max = lax.dynamic_update_slice(stat_max, row_max[:, :, 0].T, (zero_row, stat_col))
        stat_sum = lax.dynamic_update_slice(stat_sum, row_sum[:, :, 0].T, (zero_row, stat_col))
        stat_dot = lax.dynamic_update_slice(stat_dot, row_dot[:, :, 0].T, (zero_row, stat_col))
        return (
            query_grad,
            band_kgrad,
            band_vgrad,
            mem_kgrad,
            mem_vgrad,
            attn_rows,
            stat_max,
            stat_sum,
            stat_dot,
        )

    init = (
        jnp.zeros((tokens, width), jnp.float32),
        jnp.zeros((W + tokens, width), jnp.float32),
        jnp.zeros((W + tokens, width), jnp.float32),
        jnp.zeros((slot_total, width), jnp.float32),
        jnp.zeros((slot_total, width), jnp.float32),
        jnp.zeros((tokens, width), jnp.bfloat16),
        jnp.zeros((W, heads_total), jnp.float32),
        jnp.zeros((W, heads_total), jnp.float32),
        jnp.zeros((W, heads_total), jnp.float32),
    )
    (
        query_grad,
        band_kgrad,
        band_vgrad,
        mem_kgrad,
        mem_vgrad,
        attn_rows,
        stat_max,
        stat_sum,
        stat_dot,
    ) = lax.fori_loop(0, pair_count, pair_step, init)
    own_kgrad = band_kgrad[W:]
    own_vgrad = band_vgrad[W:]
    back_kgrad, back_vgrad = (
        passed_along(band_kgrad[:W].astype(jnp.bfloat16), "ctx", -1).astype(jnp.float32),
        passed_along(band_vgrad[:W].astype(jnp.bfloat16), "ctx", -1).astype(jnp.float32),
    )
    own_kgrad = own_kgrad.at[tokens - W :].add(back_kgrad)
    own_vgrad = own_vgrad.at[tokens - W :].add(back_vgrad)
    got_kgrad, got_vgrad = (
        lax.psum_scatter(
            mem_kgrad.astype(jnp.bfloat16), "ctx", scatter_dimension=0, tiled=True
        ).astype(jnp.float32),
        lax.psum_scatter(
            mem_vgrad.astype(jnp.bfloat16), "ctx", scatter_dimension=0, tiled=True
        ).astype(jnp.float32),
    )
    own_kgrad = own_kgrad.at[own_slots].add(got_kgrad)
    own_vgrad = own_vgrad.at[own_slots].add(got_vgrad)
    weight_part = lax.dot_general(
        attn_rows, grad_out, (((0,), (0,)), ((), ())), preferred_element_type=jnp.float32
    )
    weight_piece = lax.psum_scatter(
        weight_part.astype(jnp.bfloat16), "ctx", scatter_dimension=0, tiled=True
    ).astype(jnp.float32)
    weight_piece = lax.psum(weight_piece.astype(jnp.bfloat16), "fam").astype(jnp.float32)
    weight_total = lax.all_gather(
        weight_piece.astype(jnp.bfloat16), "ctx", axis=0, tiled=True
    ).astype(weight_piece.dtype)
    weight_grad = weight_total * (lax.axis_size("fam") * ctx_size * tokens) ** (-0.5)
    return (
        query_grad.astype(jnp.bfloat16)[None],
        own_kgrad.astype(jnp.bfloat16)[None],
        own_vgrad.astype(jnp.bfloat16)[None],
        weight_grad,
    )


def solution(mesh):
    return jax.shard_map(
        per_device,
        mesh=mesh,
        in_specs=(
            P("fam", "ctx", None),
            P("fam", "ctx", None),
            P("fam", "ctx", None),
            P("fam", "ctx", None),
            P(),
            P("fam", None),
            P("fam", None),
            P("fam", None),
        ),
        out_specs=(P("fam", "ctx", None), P("fam", "ctx", None), P("fam", "ctx", None), P()),
        check_vma=False,
    )
```

profile of v0, /device:TPU:3, one launch (start us, length us, event | category | flops | bytes accessed | tf_op | source)
XLA Modules:
  0.0 819.0 jit_solution(5717204973841686741)
XLA Ops:
  23.6 16.4 %all-gather = bf16[128,1024]{1,0:T(8,128)(2,1)} all-gather(bf16[16,1024]{1,0:T(8,128)(2,1)S(1)} %gather_fusion), channel_id=2, replica_groups=mesh['fam'=4,'ctx'=8] {'ctx'}, dimensions={0}, use_global_device_ids=true | all-gather | bytes 294912 | tf_op jit(solution)/shard_map/all_gather | solution.py:109
  40.0 9.5 %all-gather.1 = bf16[128,1024]{1,0:T(8,128)(2,1)} all-gather(bf16[16,1024]{1,0:T(8,128)(2,1)S(1)} %gather_fusion.1), channel_id=3, replica_groups=mesh['fam'=4,'ctx'=8] {'ctx'}, dimensions={0}, use_global_device_ids=true | all-gather | bytes 294912 | tf_op jit(solution)/shard_map/all_gather | solution.py:110
  68.6 551.9 %while.27 = (s32[]{:T(128)}, bf16[512,1024]{1,0:T(8,128)(2,1)}, f32[1024,1024]{1,0:T(8,128)}, f32[1024,1024]{1,0:T(8,128)}, f32[128,1024]{1,0:T(8,128)}, /*index...) while((s32[]{:T(128)}, bf16[512,1024]{1,0:T(8,128)(2,1)}, ...), condition=%wide.region_14.15_spmd, body=%wide.region_10.14_spmd.sunk | while | flops 935827840 | bytes 61632856 | solution.py:202
  98.0 12.6 %fusion.99 = bf16[2,64,512]{2,1,0:T(8,128)(2,1)} fusion(f32[2,512,1152]{2,1,0:T(8,128)} %fusion.97, bf16[128,2,64]{0,2,1:T(8,128)(2,1)} %bitcast.133, bf16[1024,2,64]{0,2,1:T(8,128)(2,1)} %bitcast.118, f32[2,512,1152]{2,1,0:T(8,128)} %get-tuple-element.449, f32[2,512]{1,0:T(2,128)S(1)} %broadcast_maximum_fusion.2), kind=kOutput, calls=%fused_computation.17.clone.1 | convolution fusion | flops 159844480 | bytes 9867264 | tf_op jit(solution)/shard_map/while/body/eval_jaxpr/gqk,kge->qge/dot_general | solution.py:77
  110.6 9.9 %fusion.100 = f32[1152,2,64]{0,2,1:T(8,128)} fusion(bf16[512,2,64]{0,2,1:T(8,128)(2,1)S(1)} %bitcast.123, f32[2,512,1152]{2,1,0:T(8,128)} %fusion.97, f32[2,512,1152]{2,1,0:T(8,128)} %get-tuple-element.449, f32[2,512]{1,0:T(2,128)S(1)} %broadcast_maximum_fusion.2), kind=kOutput, calls=%fused_computation.18.clone.1 | convolution fusion | flops 159254656 | bytes 10162176 | tf_op jit(solution)/shard_map/while/body/eval_jaxpr/gqk,qge->kge/dot_general | solution.py:78
  167.0 12.6 %fusion.99 = bf16[2,64,512]{2,1,0:T(8,128)(2,1)} fusion(f32[2,512,1152]{2,1,0:T(8,128)} %fusion.97, bf16[128,2,64]{0,2,1:T(8,128)(2,1)} %bitcast.133, bf16[1024,2,64]{0,2,1:T(8,128)(2,1)} %bitcast.118, f32[2,512,1152]{2,1,0:T(8,128)} %get-tuple-element.449, f32[2,512]{1,0:T(2,128)S(1)} %broadcast_maximum_fusion.2), kind=kOutput, calls=%fused_computation.17.clone.1 | convolution fusion | flops 159844480 | bytes 9867264 | tf_op jit(solution)/shard_map/while/body/eval_jaxpr/gqk,kge->qge/dot_general | solution.py:77
  179.6 9.9 %fusion.100 = f32[1152,2,64]{0,2,1:T(8,128)} fusion(bf16[512,2,64]{0,2,1:T(8,128)(2,1)S(1)} %bitcast.123, f32[2,512,1152]{2,1,0:T(8,128)} %fusion.97, f32[2,512,1152]{2,1,0:T(8,128)} %get-tuple-element.449, f32[2,512]{1,0:T(2,128)S(1)} %broadcast_maximum_fusion.2), kind=kOutput, calls=%fused_computation.18.clone.1 | convolution fusion | flops 159254656 | bytes 10162176 | tf_op jit(solution)/shard_map/while/body/eval_jaxpr/gqk,qge->kge/dot_general | solution.py:78
  236.0 12.6 %fusion.99 = bf16[2,64,512]{2,1,0:T(8,128)(2,1)} fusion(f32[2,512,1152]{2,1,0:T(8,128)} %fusion.97, bf16[128,2,64]{0,2,1:T(8,128)(2,1)} %bitcast.133, bf16[1024,2,64]{0,2,1:T(8,128)(2,1)} %bitcast.118, f32[2,512,1152]{2,1,0:T(8,128)} %get-tuple-element.449, f32[2,512]{1,0:T(2,128)S(1)} %broadcast_maximum_fusion.2), kind=kOutput, calls=%fused_computation.17.clone.1 | convolution fusion | flops 159844480 | bytes 9867264 | tf_op jit(solution)/shard_map/while/body/eval_jaxpr/gqk,kge->qge/dot_general | solution.py:77
  248.6 9.9 %fusion.100 = f32[1152,2,64]{0,2,1:T(8,128)} fusion(bf16[512,2,64]{0,2,1:T(8,128)(2,1)S(1)} %bitcast.123, f32[2,512,1152]{2,1,0:T(8,128)} %fusion.97, f32[2,512,1152]{2,1,0:T(8,128)} %get-tuple-element.449, f32[2,512]{1,0:T(2,128)S(1)} %broadcast_maximum_fusion.2), kind=kOutput, calls=%fused_computation.18.clone.1 | convolution fusion | flops 159254656 | bytes 10162176 | tf_op jit(solution)/shard_map/while/body/eval_jaxpr/gqk,qge->kge/dot_general | solution.py:78
  305.0 12.6 %fusion.99 = bf16[2,64,512]{2,1,0:T(8,128)(2,1)} fusion(f32[2,512,1152]{2,1,0:T(8,128)} %fusion.97, bf16[128,2,64]{0,2,1:T(8,128)(2,1)} %bitcast.133, bf16[1024,2,64]{0,2,1:T(8,128)(2,1)} %bitcast.118, f32[2,512,1152]{2,1,0:T(8,128)} %get-tuple-element.449, f32[2,512]{1,0:T(2,128)S(1)} %broadcast_maximum_fusion.2), kind=kOutput, calls=%fused_computation.17.clone.1 | convolution fusion | flops 159844480 | bytes 9867264 | tf_op jit(solution)/shard_map/while/body/eval_jaxpr/gqk,kge->qge/dot_general | solution.py:77
  317.6 9.9 %fusion.100 = f32[1152,2,64]{0,2,1:T(8,128)} fusion(bf16[512,2,64]{0,2,1:T(8,128)(2,1)S(1)} %bitcast.123, f32[2,512,1152]{2,1,0:T(8,128)} %fusion.97, f32[2,512,1152]{2,1,0:T(8,128)} %get-tuple-element.449, f32[2,512]{1,0:T(2,128)S(1)} %broadcast_maximum_fusion.2), kind=kOutput, calls=%fused_computation.18.clone.1 | convolution fusion | flops 159254656 | bytes 10162176 | tf_op jit(solution)/shard_map/while/body/eval_jaxpr/gqk,qge->kge/dot_general | solution.py:78
  374.0 12.6 %fusion.99 = bf16[2,64,512]{2,1,0:T(8,128)(2,1)} fusion(f32[2,512,1152]{2,1,0:T(8,128)} %fusion.97, bf16[128,2,64]{0,2,1:T(8,128)(2,1)} %bitcast.133, bf16[1024,2,64]{0,2,1:T(8,128)(2,1)} %bitcast.118, f32[2,512,1152]{2,1,0:T(8,128)} %get-tuple-element.449, f32[2,512]{1,0:T(2,128)S(1)} %broadcast_maximum_fusion.2), kind=kOutput, calls=%fused_computation.17.clone.1 | convolution fusion | flops 159844480 | bytes 9867264 | tf_op jit(solution)/shard_map/while/body/eval_jaxpr/gqk,kge->qge/dot_general | solution.py:77
  386.6 9.9 %fusion.100 = f32[1152,2,64]{0,2,1:T(8,128)} fusion(bf16[512,2,64]{0,2,1:T(8,128)(2,1)S(1)} %bitcast.123, f32[2,512,1152]{2,1,0:T(8,128)} %fusion.97, f32[2,512,1152]{2,1,0:T(8,128)} %get-tuple-element.449, f32[2,512]{1,0:T(2,128)S(1)} %broadcast_maximum_fusion.2), kind=kOutput, calls=%fused_computation.18.clone.1 | convolution fusion | flops 159254656 | bytes 10162176 | tf_op jit(solution)/shard_map/while/body/eval_jaxpr/gqk,qge->kge/dot_general | solution.py:78
  442.9 12.6 %fusion.99 = bf16[2,64,512]{2,1,0:T(8,128)(2,1)} fusion(f32[2,512,1152]{2,1,0:T(8,128)} %fusion.97, bf16[128,2,64]{0,2,1:T(8,128)(2,1)} %bitcast.133, bf16[1024,2,64]{0,2,1:T(8,128)(2,1)} %bitcast.118, f32[2,512,1152]{2,1,0:T(8,128)} %get-tuple-element.449, f32[2,512]{1,0:T(2,128)S(1)} %broadcast_maximum_fusion.2), kind=kOutput, calls=%fused_computation.17.clone.1 | convolution fusion | flops 159844480 | bytes 9867264 | tf_op jit(solution)/shard_map/while/body/eval_jaxpr/gqk,kge->qge/dot_general | solution.py:77
  455.5 9.9 %fusion.100 = f32[1152,2,64]{0,2,1:T(8,128)} fusion(bf16[512,2,64]{0,2,1:T(8,128)(2,1)S(1)} %bitcast.123, f32[2,512,1152]{2,1,0:T(8,128)} %fusion.97, f32[2,512,1152]{2,1,0:T(8,128)} %get-tuple-element.449, f32[2,512]{1,0:T(2,128)S(1)} %broadcast_maximum_fusion.2), kind=kOutput, calls=%fused_computation.18.clone.1 | convolution fusion | flops 159254656 | bytes 10162176 | tf_op jit(solution)/shard_map/while/body/eval_jaxpr/gqk,qge->kge/dot_general | solution.py:78
  511.9 12.6 %fusion.99 = bf16[2,64,512]{2,1,0:T(8,128)(2,1)} fusion(f32[2,512,1152]{2,1,0:T(8,128)} %fusion.97, bf16[128,2,64]{0,2,1:T(8,128)(2,1)} %bitcast.133, bf16[1024,2,64]{0,2,1:T(8,128)(2,1)} %bitcast.118, f32[2,512,1152]{2,1,0:T(8,128)} %get-tuple-element.449, f32[2,512]{1,0:T(2,128)S(1)} %broadcast_maximum_fusion.2), kind=kOutput, calls=%fused_computation.17.clone.1 | convolution fusion | flops 159844480 | bytes 9867264 | tf_op jit(solution)/shard_map/while/body/eval_jaxpr/gqk,kge->qge/dot_general | solution.py:77
  524.5 9.9 %fusion.100 = f32[1152,2,64]{0,2,1:T(8,128)} fusion(bf16[512,2,64]{0,2,1:T(8,128)(2,1)S(1)} %bitcast.123, f32[2,512,1152]{2,1,0:T(8,128)} %fusion.97, f32[2,512,1152]{2,1,0:T(8,128)} %get-tuple-element.449, f32[2,512]{1,0:T(2,128)S(1)} %broadcast_maximum_fusion.2), kind=kOutput, calls=%fused_computation.18.clone.1 | convolution fusion | flops 159254656 | bytes 10162176 | tf_op jit(solution)/shard_map/while/body/eval_jaxpr/gqk,qge->kge/dot_general | solution.py:78
  580.9 12.6 %fusion.99 = bf16[2,64,512]{2,1,0:T(8,128)(2,1)} fusion(f32[2,512,1152]{2,1,0:T(8,128)} %fusion.97, bf16[128,2,64]{0,2,1:T(8,128)(2,1)} %bitcast.133, bf16[1024,2,64]{0,2,1:T(8,128)(2,1)} %bitcast.118, f32[2,512,1152]{2,1,0:T(8,128)} %get-tuple-element.449, f32[2,512]{1,0:T(2,128)S(1)} %broadcast_maximum_fusion.2), kind=kOutput, calls=%fused_computation.17.clone.1 | convolution fusion | flops 159844480 | bytes 9867264 | tf_op jit(solution)/shard_map/while/body/eval_jaxpr/gqk,kge->qge/dot_general | solution.py:77
  593.5 9.9 %fusion.100 = f32[1152,2,64]{0,2,1:T(8,128)} fusion(bf16[512,2,64]{0,2,1:T(8,128)(2,1)S(1)} %bitcast.123, f32[2,512,1152]{2,1,0:T(8,128)} %fusion.97, f32[2,512,1152]{2,1,0:T(8,128)} %get-tuple-element.449, f32[2,512]{1,0:T(2,128)S(1)} %broadcast_maximum_fusion.2), kind=kOutput, calls=%fused_computation.18.clone.1 | convolution fusion | flops 159254656 | bytes 10162176 | tf_op jit(solution)/shard_map/while/body/eval_jaxpr/gqk,qge->kge/dot_general | solution.py:78
  624.6 41.7 %reduce-scatter.8.cloned.1.call-done = bf16[128,1024]{1,0:T(8,128)(2,1)} async-done(((bf16[1024,1024]{1,0:T(8,128)(2,1)}), bf16[128,1024]{1,0:T(8,128)(2,1)}) %reduce-scatter.8.cloned.1.call-update) | async-done | bytes 262160 | tf_op jit(solution)/shard_map/reduce_scatter | solution.py:224
  670.1 32.5 %all-reduce.2.cloned.1.call-done = bf16[128,1024]{1,0:T(8,128)(2,1)} async-done(((bf16[128,1024]{1,0:T(8,128)(2,1)}), bf16[128,1024]{1,0:T(8,128)(2,1)}) %all-reduce.2.cloned.1.call-update) | async-done | bytes 262160 | tf_op jit(solution)/shard_map/psum | solution.py:227
  724.2 16.4 %reduce-scatter.6.cloned.1.call-done = bf16[16,1024]{1,0:T(8,128)(2,1)} async-done(((bf16[128,1024]{1,0:T(8,128)(2,1)}), bf16[16,1024]{1,0:T(8,128)(2,1)}) %reduce-scatter.6.cloned.1.call-update) | async-done | bytes 32784 | tf_op jit(solution)/shard_map/reduce_scatter | solution.py:215
  747.7 30.0 %reduce-scatter.4.cloned.1.call-done = bf16[16,1024]{1,0:T(8,128)(2,1)} async-done(((bf16[128,1024]{1,0:T(8,128)(2,1)}), bf16[16,1024]{1,0:T(8,128)(2,1)}) %reduce-scatter.4.cloned.1.call-update) | async-done | bytes 32784 | tf_op jit(solution)/shard_map/reduce_scatter | solution.py:212
  785.5 22.7 %all-gather.4.cloned.1.call-done = bf16[1024,1024]{1,0:T(8,128)(2,1)} async-done(((bf16[128,1024]{1,0:T(8,128)(2,1)}), bf16[1024,1024]{1,0:T(8,128)(2,1)}) %all-gather.4.cloned.1.call-update) | async-done | bytes 2097168 | tf_op jit(solution)/shard_map/all_gather | solution.py:228
  (441 shorter events, 455.0 us)
Async XLA Ops:
  7.2 44.4 %copy-start = (bf16[1024,1024]{1,0:T(8,128)(2,1)S(1)}, bf16[1024,1024]{1,0:T(8,128)(2,1)}, u32[]{:S(2)}) copy-start(bf16[1024,1024]{1,0:T(8,128)(2,1)} %param.22) | copy-start | bytes 6291460
  7.2 659.2 %reduce-scatter.8.cloned.1.call-start = ((), (), s32[]{:S(2)}) async-start(), calls=%async_computation.5 | async-start | bytes 2359296 | tf_op jit(solution)/shard_map/reduce_scatter | solution.py:224
  7.2 48.0 %collective-permute-start = (bf16[512,1024]{1,0:T(8,128)(2,1)}, bf16[512,1024]{1,0:T(8,128)(2,1)}, u32[]{:S(2)}, u32[]{:S(2)}) collective-permute-start(bf16[512,1024]{1,0:T(8,128)(2,1)} %bitcast.125), channel_id=1, source_target_pairs={{0,1},{1,2},{2,3},{3,4},{4,5},{5,6},{6,7},{8,9},{9,10},{10,11},{11... | collective-permute-start | bytes 3145736 | tf_op jit(solution)/shard_map/ppermute | solution.py:17
  11.0 47.1 %collective-permute-start.1 = (bf16[512,1024]{1,0:T(8,128)(2,1)}, bf16[512,1024]{1,0:T(8,128)(2,1)S(1)}, u32[]{:S(2)}, u32[]{:S(2)}) collective-permute-start(bf16[512,1024]{1,0:T(8,128)(2,1)} %bitcast.128), channel_id=1, source_target_pairs={{0,1},{1,2},{2,3},{3,4},{4,5},{5,6},{6,7},{8,9},{9,10},{10,11},{11... | collective-permute-start | bytes 3145736 | tf_op jit(solution)/shard_map/ppermute | solution.py:17
  98.0 12.6 %copy-start.4 = (bf16[512,128]{0,1:T(8,128)(2,1)S(1)}, bf16[512,128]{0,1:T(8,128)(2,1)}, u32[]{:S(2)}) copy-start(bf16[512,128]{0,1:T(8,128)(2,1)} %constant_dynamic-slice_fusion.25) | copy-start | bytes 393220 | tf_op jit(solution)/shard_map/while
  124.3 8.0 copy-start.3
  167.0 12.6 %copy-start.4 = (bf16[512,128]{0,1:T(8,128)(2,1)S(1)}, bf16[512,128]{0,1:T(8,128)(2,1)}, u32[]{:S(2)}) copy-start(bf16[512,128]{0,1:T(8,128)(2,1)} %constant_dynamic-slice_fusion.25) | copy-start | bytes 393220 | tf_op jit(solution)/shard_map/while
  236.0 12.6 %copy-start.4 = (bf16[512,128]{0,1:T(8,128)(2,1)S(1)}, bf16[512,128]{0,1:T(8,128)(2,1)}, u32[]{:S(2)}) copy-start(bf16[512,128]{0,1:T(8,128)(2,1)} %constant_dynamic-slice_fusion.25) | copy-start | bytes 393220 | tf_op jit(solution)/shard_map/while
  262.2 8.0 copy-start.3
  305.0 12.6 %copy-start.4 = (bf16[512,128]{0,1:T(8,128)(2,1)S(1)}, bf16[512,128]{0,1:T(8,128)(2,1)}, u32[]{:S(2)}) copy-start(bf16[512,128]{0,1:T(8,128)(2,1)} %constant_dynamic-slice_fusion.25) | copy-start | bytes 393220 | tf_op jit(solution)/shard_map/while
  374.0 12.6 %copy-start.4 = (bf16[512,128]{0,1:T(8,128)(2,1)S(1)}, bf16[512,128]{0,1:T(8,128)(2,1)}, u32[]{:S(2)}) copy-start(bf16[512,128]{0,1:T(8,128)(2,1)} %constant_dynamic-slice_fusion.25) | copy-start | bytes 393220 | tf_op jit(solution)/shard_map/while
  400.2 8.0 copy-start.3
  442.9 12.6 %copy-start.4 = (bf16[512,128]{0,1:T(8,128)(2,1)S(1)}, bf16[512,128]{0,1:T(8,128)(2,1)}, u32[]{:S(2)}) copy-start(bf16[512,128]{0,1:T(8,128)(2,1)} %constant_dynamic-slice_fusion.25) | copy-start | bytes 393220 | tf_op jit(solution)/shard_map/while
  469.2 8.0 copy-start.3
  511.9 12.6 %copy-start.4 = (bf16[512,128]{0,1:T(8,128)(2,1)S(1)}, bf16[512,128]{0,1:T(8,128)(2,1)}, u32[]{:S(2)}) copy-start(bf16[512,128]{0,1:T(8,128)(2,1)} %constant_dynamic-slice_fusion.25) | copy-start | bytes 393220 | tf_op jit(solution)/shard_map/while
  538.2 8.0 copy-start.3
  580.9 12.6 %copy-start.4 = (bf16[512,128]{0,1:T(8,128)(2,1)S(1)}, bf16[512,128]{0,1:T(8,128)(2,1)}, u32[]{:S(2)}) copy-start(bf16[512,128]{0,1:T(8,128)(2,1)} %constant_dynamic-slice_fusion.25) | copy-start | bytes 393220 | tf_op jit(solution)/shard_map/while
  624.6 78.0 %all-reduce.2.cloned.1.call-start = ((), (), s32[]{:S(2)}) async-start(), calls=%async_computation.6 | async-start | bytes 524288 | tf_op jit(solution)/shard_map/psum | solution.py:227
  666.4 74.2 %reduce-scatter.6.cloned.1.call-start = ((), (), s32[]{:S(2)}) async-start(), calls=%async_computation.4 | async-start | bytes 294912 | tf_op jit(solution)/shard_map/reduce_scatter | solution.py:215
  668.2 109.5 %reduce-scatter.4.cloned.1.call-start = ((), (), s32[]{:S(2)}) async-start(), calls=%async_computation.3 | async-start | bytes 294912 | tf_op jit(solution)/shard_map/reduce_scatter | solution.py:212
  670.1 138.2 %all-gather.4.cloned.1.call-start = ((), (), s32[]{:S(2)}) async-start(), calls=%async_computation.7 | async-start | bytes 2359296 | tf_op jit(solution)/shard_map/all_gather | solution.py:228
  702.6 19.9 %copy-start.1 = (f32[1024,1024]{1,0:T(8,128)S(1)}, f32[1024,1024]{1,0:T(8,128)}, u32[]{:S(2)}) copy-start(f32[1024,1024]{1,0:T(8,128)} %get-tuple-element.281) | copy-start | bytes 12582916
  704.6 18.0 %collective-permute-start.3 = (bf16[512,1024]{1,0:T(8,128)(2,1)S(1)}, bf16[512,1024]{1,0:T(8,128)(2,1)S(1)}, u32[]{:S(2)}, u32[]{:S(2)}) collective-permute-start(bf16[512,1024]{1,0:T(8,128)(2,1)S(1)} %slice.88), channel_id=1, source_target_pairs={{1,0},{2,1},{3,2},{4,3},{5,4},{6,5},{7,6},{9,8},{10,9},{11,10},{12... | collective-permute-start | bytes 3145736 | tf_op jit(solution)/shard_map/ppermute | solution.py:17
  711.7 32.7 %collective-permute-start.2 = (bf16[512,1024]{1,0:T(8,128)(2,1)}, bf16[512,1024]{1,0:T(8,128)(2,1)S(1)}, u32[]{:S(2)}, u32[]{:S(2)}) collective-permute-start(bf16[512,1024]{1,0:T(8,128)(2,1)} %slice.89), channel_id=1, source_target_pairs={{1,0},{2,1},{3,2},{4,3},{5,4},{6,5},{7,6},{9,8},{10,9},{11,10},{12... | collective-permute-start | bytes 3145736 | tf_op jit(solution)/shard_map/ppermute | solution.py:17
  (15 other events, 100.2 us)
Sparse Core Ops, SparseCore 0:
  624.7 41.5 reduce-scatter.7
  668.7 33.9 all-reduce.1
  705.6 34.8 reduce-scatter.5
  744.0 33.6 reduce-scatter.3
  779.5 28.7 all-gather.3
where the time goes:
time: 828 us; the launch traced here: 819 us
  matrix products  325 us (39%)
  local copies, waits for them, and re-layouts  233 us (28%)
  waiting for transfers between devices  152 us (18%)
  other arithmetic  55.8 us (7%)
  blocking collectives  25.9 us (3%)
  between operations  13.9 us (2%)
  starting transfers between devices  12.3 us (1%)
    dot_general x8, matrix products, attend(): jnp.einsum('gqk,kge->qge', grad_score, key_blk, preferred_element_type=jn...  101 us
    dot_general x8, matrix products, attend(): jnp.einsum('gqk,qge->kge', grad_score, query_blk, preferred_element_type=...  79.1 us
    dynamic_slice x88, local copies, waits for them, and re-layouts, columns_of(): return lax.dynamic_slice_in_dim(array, column, span, 1)  67.7 us
    dynamic_slice x64, local copies, waits for them, and re-layouts, add_into(): current = lax.dynamic_slice(target, (row_index, column), update.shape)  60.2 us
    sub x8, matrix products, attend(): expo = jnp.where(live, jnp.exp(shifted - row_max), 0.0)  46.3 us
    reduce_scatter x1, waiting for transfers between devices, per_device(): lax.psum_scatter(weight_part.astype(jnp.bfloat16), 'ctx', scatter_dimensi...  41.7 us
    dynamic_update_slice x48, local copies, waits for them, and re-layouts, add_into(): lax.dynamic_update_slice(target, current + update, (row_index, column))  34.9 us
    psum x1, waiting for transfers between devices, per_device(): lax.psum(weight_piece.astype(jnp.bfloat16), 'fam').astype(jnp.float32)  32.5 us
  transfers between devices with their start and end apart: 9, of which 6 were waited for; matrix products, arithmetic and copies ran while one was open for 5% of the time, Pallas kernels for 0%

commit v1 on v0

v1 whole, which is shorter than its diff:
```python
import functools
import jax, jax.numpy as jnp
from jax import lax
from jax.experimental import pallas as pl
from jax.experimental.pallas import tpu as pltpu
HEAD_DIM=64; W=512; BLK=128; NEG=-1e30
NT=(((1,),(1,)),((),())); NN=(((1,),(0,)),((),())); TN=(((0,),(0,)),((),()))
f32=jnp.float32; bf16=jnp.bfloat16
def dot(a,b,d): return lax.dot_general(a,b,d,preferred_element_type=f32)

def attn_kernel(info_ref, q_ref, g_ref, ko_ref, vo_ref, kh_ref, vh_ref, km_ref, vm_ref, mb_ref,
                dq_ref, at_ref, dko_ref, dvo_ref, dkh_ref, dvh_ref, dkm_ref, dvm_ref,
                ke, ve, q2, g2, pt, dst, *, nb, far):
    slots = km_ref.shape[0]
    span = 2*HEAD_DIM
    hrows = kh_ref.shape[0]; orows = ko_ref.shape[0]
    ext = hrows+orows
    two = 2*BLK
    ke[0:hrows,:] = kh_ref[...]; ke[hrows:ext,:] = ko_ref[...]; ke[ext:,:] = km_ref[...]
    ve[0:hrows,:span] = vh_ref[...]; ve[hrows:ext,:span] = vo_ref[...]; ve[ext:,:span] = vm_ref[...]
    ve[:, span:] = jnp.ones((ext+slots, span), bf16)
    lane = lax.broadcasted_iota(jnp.int32,(BLK,span),1)
    first = lane < HEAD_DIM
    kk = lax.broadcasted_iota(jnp.int32,(BLK,two),0)
    qq = lax.broadcasted_iota(jnp.int32,(BLK,two),1) % BLK
    tri = kk <= qq
    lane2 = lax.broadcasted_iota(jnp.int32,(two,span),1)
    row2 = lax.broadcasted_iota(jnp.int32,(two,span),0) % BLK
    zero = jnp.zeros((BLK,span),bf16)
    for b in range(nb):
        rows = slice(b*BLK,(b+1)*BLK); r2 = slice(b*two,(b+1)*two)
        q = q_ref[rows,:]*jnp.asarray(HEAD_DIM**-0.5,bf16)
        q2b = jnp.concatenate([jnp.where(first,q,zero), jnp.where(first,zero,q)],0)
        q2[r2,:] = q2b
        s = dot(ke[b*BLK:(b+far+1)*BLK,:], q2b, NT)
        sm = dot(ke[ext:,:], q2b, NT) + jnp.concatenate([mb_ref[b],mb_ref[b]],1)
        lo = info_ref[0,b]
        off = [jnp.where(e+b >= lo, 0.0, NEG).astype(f32) for e in range(far)]
        s0 = jnp.where(tri, s[far*BLK:,:], s[:BLK,:]+off[0])
        mid = [s[e*BLK:(e+1)*BLK,:] for e in range(1,far)]
        m = jnp.maximum(jnp.max(s0,0,keepdims=True), jnp.max(sm,0,keepdims=True))
        for e in range(1,far):
            m = jnp.maximum(m, jnp.max(mid[e-1],0,keepdims=True)+off[e])
        p0 = jnp.exp(s0-m).astype(bf16)
        zb = jnp.zeros_like(p0)
        pt[b*BLK:(b+1)*BLK, r2] = jnp.where(tri, zb, p0)
        pt[(b+far)*BLK:(b+far+1)*BLK, r2] = jnp.where(tri, p0, zb)
        for e in range(1,far):
            pt[(b+e)*BLK:(b+e+1)*BLK, r2] = jnp.exp(mid[e-1]-(m-off[e])).astype(bf16)
        pt[ext:, r2] = jnp.exp(sm-m).astype(bf16)
        o = dot(pt[b*BLK:(b+far+1)*BLK, r2], ve[b*BLK:(b+far+1)*BLK,:], TN) + dot(pt[ext:, r2], ve[ext:,:], TN)
        scale = jnp.where(row2 < info_ref[1,b], 1.0/o[:,span:], 0.0)
        on = o[:,:span]*scale
        at_ref[rows,:] = jnp.where(first, on[:BLK], on[BLK:]).astype(bf16)
        g = g_ref[rows,:].astype(f32)
        gz = jnp.zeros_like(g)
        g2f = jnp.concatenate([jnp.where(first,g,gz), jnp.where(first,gz,g)],0)*scale
        g2b = g2f.astype(bf16)
        g2[r2,:] = g2b
        dd = -jnp.sum(g2b.astype(f32)*on,1,keepdims=True)
        dhi = dd.astype(bf16).astype(f32)
        daug = jnp.where(lane2==0, dhi, jnp.where(lane2==1, dd-dhi, 0.0)).astype(bf16)
        gaug = jnp.concatenate([g2b,daug],1)
        dp = dot(ve[b*BLK:(b+far+1)*BLK,:], gaug, NT)
        dst[b*BLK:(b+far+1)*BLK, r2] = (pt[b*BLK:(b+far+1)*BLK, r2].astype(f32)*dp).astype(bf16)
        dpm = dot(ve[ext:,:], gaug, NT)
        dst[ext:, r2] = (pt[ext:, r2].astype(f32)*dpm).astype(bf16)
        dq = dot(dst[b*BLK:(b+far+1)*BLK, r2], ke[b*BLK:(b+far+1)*BLK,:], TN) + dot(dst[ext:, r2], ke[ext:,:], TN)
        dq_ref[rows,:] = (jnp.where(first, dq[:BLK], dq[BLK:])*(HEAD_DIM**-0.5)).astype(bf16)
    hb = hrows//BLK
    for e in range(ext//BLK):
        b0, b1 = max(0,e-far), min(nb-1,e)
        cr = slice(b0*two,(b1+1)*two)
        er = slice(e*BLK,(e+1)*BLK)
        dv = dot(pt[er,cr], g2[cr,:], NN)
        dk = dot(dst[er,cr], q2[cr,:], NN)
        if e < hb:
            dvh_ref[er,:] = dv.astype(bf16); dkh_ref[er,:] = dk.astype(bf16)
        else:
            orr = slice((e-hb)*BLK,(e-hb+1)*BLK)
            dvo_ref[orr,:] = dv; dko_ref[orr,:] = dk
    dvm_ref[...] = dot(pt[ext:,:], g2[...], NN).astype(bf16)
    dkm_ref[...] = dot(dst[ext:,:], q2[...], NN).astype(bf16)

def attn(info, q, g, ko, vo, kh, vh, km, vm, mb, *, p0=0, np_=None):
    tokens, width = q.shape; slots = km.shape[0]
    nb = tokens//BLK; far = W//BLK; span=2*HEAD_DIM
    np_ = np_ or width//span
    ext = kh.shape[0]+tokens
    col = lambda r: pl.BlockSpec((r,span), lambda p,*_: (0,p+p0))
    ocol = lambda r: pl.BlockSpec((r,span), lambda p,*_: (0,p))
    hw = np_*span
    outs = [((tokens,hw),bf16),((tokens,hw),bf16),((tokens,hw),f32),((tokens,hw),f32),
            ((kh.shape[0],hw),bf16),((kh.shape[0],hw),bf16),((slots,hw),bf16),((slots,hw),bf16)]
    return pl.pallas_call(
        functools.partial(attn_kernel, nb=nb, far=far),
        grid_spec=pltpu.PrefetchScalarGridSpec(
            num_scalar_prefetch=1, grid=(np_,),
            in_specs=[col(tokens),col(tokens),col(tokens),col(tokens),col(kh.shape[0]),col(kh.shape[0]),col(slots),col(slots),
                      pl.BlockSpec(mb.shape, lambda p,*_:(0,0,0))],
            out_specs=[ocol(s[0]) for s,_ in outs],
            scratch_shapes=[pltpu.VMEM((ext+slots,span),bf16), pltpu.VMEM((ext+slots,2*span),bf16),
                            pltpu.VMEM((nb*2*BLK,span),bf16), pltpu.VMEM((nb*2*BLK,span),bf16),
                            pltpu.VMEM((ext+slots,nb*2*BLK),bf16), pltpu.VMEM((ext+slots,nb*2*BLK),bf16)]),
        out_shape=[jax.ShapeDtypeStruct(s,d) for s,d in outs],
        compiler_params=pltpu.CompilerParams(vmem_limit_bytes=48<<20),
        name="band_grad",
    )(info, q, g, ko, vo, kh, vh, km, vm, mb)


from jax.sharding import PartitionSpec as P


def protein_tables(prot_blocks, last_fill):
    prot_ends = jnp.cumsum(prot_blocks)
    starts = prot_ends - prot_blocks
    valid_len = (prot_blocks - 1) * BLK + last_fill
    return prot_ends, starts, valid_len


def token_info(positions, tables):
    prot_ends, starts, valid_len = tables
    count = prot_ends.shape[0]
    blocks = jnp.floor_divide(positions, BLK)
    protein = jnp.sum((blocks[:, None] >= prot_ends[None, :]).astype(jnp.int32), axis=1)
    onehot = protein[:, None] == jnp.arange(count, dtype=jnp.int32)[None, :]
    first = jnp.sum(jnp.where(onehot, starts[None, :], 0), axis=1)
    length = jnp.sum(jnp.where(onehot, valid_len[None, :], 0), axis=1)
    left = length - (positions - first * BLK)
    return protein, first, left


def swap(x, axis, bit):
    n = lax.axis_size(axis)
    return lax.ppermute(x, axis, [(i, i ^ bit) for i in range(n)])


def bits_of(n):
    out, b = [], 1
    while b < n:
        out.append(b)
        b *= 2
    return out


def gather_rows(x, axis):
    me = lax.axis_index(axis)
    for bit in bits_of(lax.axis_size(axis)):
        other = swap(x, axis, bit)
        upper = (me & bit) != 0
        x = jnp.where(upper, jnp.concatenate([other, x], 0), jnp.concatenate([x, other], 0))
    return x


def scatter_rows(x, axis):
    me = lax.axis_index(axis)
    for bit in reversed(bits_of(lax.axis_size(axis))):
        half = x.shape[0] // 2
        upper = (me & bit) != 0
        lo, hi = x[:half], x[half:]
        keep = jnp.where(upper, hi, lo)
        send = jnp.where(upper, lo, hi)
        x = keep.astype(f32) + swap(send.astype(bf16), axis, bit).astype(f32)
    return x


def per_device(queries, key_rows, value_rows, cotangent, out_weight, prot_blocks, last_fill, memory_slots):
    q, k, v, cot = queries[0], key_rows[0], value_rows[0], cotangent[0]
    tables = protein_tables(prot_blocks[0], last_fill[0])
    slots = memory_slots[0]
    tokens, width = q.shape
    nctx = lax.axis_size("ctx")
    me = lax.axis_index("ctx")
    total = slots.shape[0]
    mine = total // nctx
    nb = tokens // BLK
    own_slots = lax.dynamic_slice_in_dim(slots, me * mine, mine)
    mem = gather_rows(jnp.concatenate([k[own_slots], v[own_slots]], 1), "ctx")
    shift = [(i, i + 1) for i in range(nctx - 1)]
    kh, vh = lax.ppermute(k, "ctx", shift), lax.ppermute(v, "ctx", shift)
    grad_attn = jnp.einsum("te,de->td", cot, out_weight, preferred_element_type=f32).astype(bf16)
    heads = me * tokens + jnp.arange(nb, dtype=jnp.int32) * BLK
    prot_q, first_q, left_q = token_info(heads, tables)
    lo = jnp.clip(first_q - (me * tokens - W) // BLK, 0, 2 * W)
    info = jnp.stack([lo, jnp.clip(left_q, 0, BLK)])
    source = jnp.arange(total, dtype=jnp.int32) // mine * tokens + slots
    prot_m, _, left_m = token_info(source, tables)
    seen = (left_m > 0)[None, :] & (prot_m[None, :] < prot_q[:, None])
    bias = jnp.broadcast_to(jnp.where(seen, 0.0, NEG).astype(f32)[:, :, None], (nb, total, BLK))
    dq, att, dko, dvo, dkh, dvh, dkm, dvm = attn(
        info, q, grad_attn, k, v, kh, vh, mem[:, :width], mem[:, width:], bias)
    weight = lax.dot_general(att, cot, TN, preferred_element_type=f32)
    piece = scatter_rows(scatter_rows(weight, "ctx"), "fam")
    scale = (lax.axis_size("fam") * nctx * tokens) ** -0.5
    weight = gather_rows(gather_rows(piece.astype(bf16), "fam"), "ctx").astype(f32) * scale
    back = [(i + 1, i) for i in range(nctx - 1)]
    bk, bv = lax.ppermute(dkh, "ctx", back), lax.ppermute(dvh, "ctx", back)
    dmem = scatter_rows(jnp.concatenate([dkm, dvm], 1), "ctx")
    pick = (jnp.arange(tokens, dtype=jnp.int32)[:, None] == own_slots[None, :]).astype(bf16)
    dmem = jnp.dot(pick, dmem.astype(bf16), preferred_element_type=f32)
    dk = (dko + bk.astype(f32) + dmem[:, :width]).astype(bf16)
    dv = (dvo + bv.astype(f32) + dmem[:, width:]).astype(bf16)
    return dq[None], dk[None], dv[None], weight


def solution(mesh):
    row = P("fam", "ctx", None)
    small = P("fam", None)
    return jax.shard_map(
        per_device,
        mesh=mesh,
        in_specs=(row, row, row, row, P(), small, small, small),
        out_specs=(row, row, row, P()),
        check_vma=False,
    )
```

time: 828 us -> 222 us (0.27); the launches traced: 819 us -> 222 us
  matrix products: 325 us -> 5.46 us
  local copies, waits for them, and re-layouts: 233 us -> 5.3 us
  Pallas kernels: 0 us -> 51.9 us
  waiting for transfers between devices: 152 us -> 107 us
  other arithmetic: 55.8 us -> 16.1 us
  blocking collectives: 25.9 us -> 0 us
  starting transfers between devices: 12.3 us -> 35 us
  between operations: 13.9 us -> 1.07 us
    dot_general x42 -> x3, matrix products: 279 us -> 5.46 us  [the longest x1 3.49 us: per_device(): jnp.einsum('te,de->td', cot, out_weight, preferred_element_type=f32)]
    dynamic_slice x152 -> x0, local copies, waits for them, and re-layouts: 128 us -> none  [the longest x88 67.7 us: columns_of(): return lax.dynamic_slice_in_dim(array, column, span, 1)]
    ppermute x4 -> x20, waiting for transfers between devices: 8.91 us -> 107 us  [the longest x16 87.8 us: swap(): return lax.ppermute(x, axis, [(i, i ^ bit) for i in range(n)])]
    reduce_scatter x3 -> x0, waiting for transfers between devices: 88.1 us -> none  [the longest x1 41.7 us: per_device(): lax.psum_scatter(weight_part.astype(jnp.bfloat16), 'ctx', scatter_dimensi...]
    dynamic_update_slice x72 -> x0, local copies, waits for them, and re-layouts: 61.2 us -> none  [the longest x48 34.9 us: add_into(): lax.dynamic_update_slice(target, current + update, (row_index, column))]
    pallas_call x0 -> x1, Pallas kernels: none -> 51.9 us  [attn(): pl.pallas_call(functools.partial(attn_kernel, nb=nb, far=far), grid_spec=...]
    sub x8 -> x0, matrix products: 46.3 us -> none  [attend(): expo = jnp.where(live, jnp.exp(shifted - row_max), 0.0)]
    psum x1 -> x0, waiting for transfers between devices: 32.5 us -> none  [per_device(): lax.psum(weight_piece.astype(jnp.bfloat16), 'fam').astype(jnp.float32)]
  transfers between devices with their start and end apart: 9 -> 20, of which waited for: 6 -> 13; matrix products, arithmetic and copies ran while one was open for 5% -> 8% of each run, Pallas kernels for 0% -> 0%
where the time goes in v1:
time: 222 us
  waiting for transfers between devices  107 us (48%)
  Pallas kernels  51.9 us (23%)
  starting transfers between devices  35 us (16%)
  other arithmetic  16.1 us (7%)
  matrix products  5.46 us (2%)
  local copies, waits for them, and re-layouts  5.3 us (2%)
    ppermute x16, waiting for transfers between devices, swap(): return lax.ppermute(x, axis, [(i, i ^ bit) for i in range(n)])  87.8 us
    pallas_call x1, Pallas kernels, attn(): pl.pallas_call(functools.partial(attn_kernel, nb=nb, far=far), grid_spec=...  51.9 us
    ppermute x16, starting transfers between devices, swap(): return lax.ppermute(x, axis, [(i, i ^ bit) for i in range(n)])  24.4 us
    ppermute x2, waiting for transfers between devices, per_device(): bk, bv = (lax.ppermute(dkh, 'ctx', back), lax.ppermute(dvh, 'ctx', back))  19.1 us
    ppermute x2, starting transfers between devices, per_device(): kh, vh = (lax.ppermute(k, 'ctx', shift), lax.ppermute(v, 'ctx', shift))  5.74 us
    ppermute x2, starting transfers between devices, per_device(): bk, bv = (lax.ppermute(dkh, 'ctx', back), lax.ppermute(dvh, 'ctx', back))  4.79 us
  transfers between devices with their start and end apart: 20, of which 13 were waited for; matrix products, arithmetic and copies ran while one was open for 8% of the time, Pallas kernels for 0%

profile of v1, /device:TPU:3, one launch (start us, length us, event | category | flops | bytes accessed | tf_op | source)
XLA Modules:
  0.0 221.8 jit_solution(16027750801618048382)
XLA Ops:
  0.6 3.8 %collective-permute-start = (bf16[512,1024]{1,0:T(8,128)(2,1)}, bf16[512,1024]{1,0:T(8,128)(2,1)}, u32[]{:S(2)}, u32[]{:S(2)}) collective-permute-start(bf16[512,1024]{1,0:T(8,128)(2,1)} %bitcast.56), channel_id=1, source_target_pairs={{0,1},{1,2},{2,3},{3,4},{4,5},{5,6},{6,7},{8,9},{9,10},{10,11},{11... | collective-permute-start | bytes 3145736 | tf_op jit(solution)/shard_map/ppermute | solution.py:180
  9.1 2.0 gather_fusion.1
  14.4 3.5 %convolution_convert_fusion.g_ref = bf16[512,1024]{1,0:T(8,128)(2,1)} fusion(bf16[1024,1024]{1,0:T(8,128)(2,1)S(1)} %copy-done, bf16[1,512,1024]{2,1,0:T(8,128)(2,1)} %param.11), kind=kOutput, calls=%fused_computation.10 | convolution fusion | flops 1074266112 | bytes 4194304 | tf_op jit(solution)/shard_map/te,de->td/dot_general | solution.py:181
  19.8 11.7 %collective-permute-done.3 = bf16[32,2048]{1,0:T(8,128)(2,1)} collective-permute-done((bf16[32,2048]{1,0:T(8,128)(2,1)S(1)}, bf16[32,2048]{1,0:T(8,128)(2,1)}, u32[]{:S(2)}, u32[]{:S(2)}) %collective-permute-start.3) | collective-permute-done | bytes 131104 | tf_op jit(solution)/shard_map/ppermute | solution.py:135
  34.3 3.6 %collective-permute-done.4 = bf16[64,2048]{1,0:T(8,128)(2,1)} collective-permute-done((bf16[64,2048]{1,0:T(8,128)(2,1)S(1)}, bf16[64,2048]{1,0:T(8,128)(2,1)}, u32[]{:S(2)}, u32[]{:S(2)}) %collective-permute-start.4) | collective-permute-done | bytes 262176 | tf_op jit(solution)/shard_map/ppermute | solution.py:135
  39.3 51.9 %band_grad.1 = (bf16[512,1024]{1,0:T(8,128)(2,1)}, bf16[512,1024]{1,0:T(8,128)(2,1)S(1)}, f32[512,1024]{1,0:T(8,128)}, f32[512,1024]{1,0:T(8,128)}, bf16[512,102...) custom-call(s32[2,4]{1,0:T(2,128)S(1)} %pad_add_fusion.info_ref, ...), custom_call_target="tpu_custom_call" | custom-call | tf_op jit(solution)/shard_map/band_grad/pallas_call | solution.py:95
  93.9 18.6 %collective-permute-done.10 = bf16[512,1024]{1,0:T(8,128)(2,1)S(1)} collective-permute-done((bf16[512,1024]{1,0:T(8,128)(2,1)S(1)}, bf16[512,1024]{1,0:T(8,128)(2,1)S(1)}, u32[]{:S(2)}, u32[]{:S(2)}) %collective-permute-start.10) | collective-permute-done | bytes 1048608 | tf_op jit(solution)/shard_map/ppermute | solution.py:135
  115.2 9.6 %collective-permute-done.11 = bf16[256,1024]{1,0:T(8,128)(2,1)S(1)} collective-permute-done((bf16[256,1024]{1,0:T(8,128)(2,1)S(1)}, bf16[256,1024]{1,0:T(8,128)(2,1)S(1)}, u32[]{:S(2)}, u32[]{:S(2)}) %collective-permute-start.11) | collective-permute-done | bytes 524320 | tf_op jit(solution)/shard_map/ppermute | solution.py:135
  129.0 2.4 %collective-permute-start.13 = (bf16[64,1024]{1,0:T(8,128)(2,1)S(1)}, bf16[64,1024]{1,0:T(8,128)(2,1)S(1)}, u32[]{:S(2)}, u32[]{:S(2)}) collective-permute-start(bf16[64,1024]{1,0:T(8,128)(2,1)S(1)} %select_convert_fusion.3), channel_id=1, source_target_pairs={{0,16},{8,24},{16,0},{24,8},{1,17},{9,25},{17,1},{25,9},{2,18},{10... | collective-permute-start | bytes 393224 | tf_op jit(solution)/shard_map/ppermute | solution.py:135
  131.4 6.3 %collective-permute-done.13 = bf16[64,1024]{1,0:T(8,128)(2,1)S(1)} collective-permute-done((bf16[64,1024]{1,0:T(8,128)(2,1)S(1)}, bf16[64,1024]{1,0:T(8,128)(2,1)S(1)}, u32[]{:S(2)}, u32[]{:S(2)}) %collective-permute-start.13) | collective-permute-done | bytes 131104 | tf_op jit(solution)/shard_map/ppermute | solution.py:135
  138.8 2.3 %collective-permute-start.6 = (bf16[64,2048]{1,0:T(8,128)(2,1)S(1)}, bf16[64,2048]{1,0:T(8,128)(2,1)S(1)}, u32[]{:S(2)}, u32[]{:S(2)}) collective-permute-start(bf16[64,2048]{1,0:T(8,128)(2,1)S(1)} %broadcast_select_fusion), channel_id=1, source_target_pairs={{0,4},{1,5},{2,6},{3,7},{4,0},{5,1},{6,2},{7,3},{8,12},{9,13},{10,... | collective-permute-start | bytes 786440 | tf_op jit(solution)/shard_map/ppermute | solution.py:135
  142.0 2.6 %collective-permute-done.15 = bf16[32,1024]{1,0:T(8,128)(2,1)S(1)} collective-permute-done((bf16[32,1024]{1,0:T(8,128)(2,1)S(1)}, bf16[32,1024]{1,0:T(8,128)(2,1)S(1)}, u32[]{:S(2)}, u32[]{:S(2)}) %collective-permute-start.15) | collective-permute-done | bytes 65568 | tf_op jit(solution)/shard_map/ppermute | solution.py:135
  144.6 3.2 %collective-permute-start.16 = (bf16[64,1024]{1,0:T(8,128)(2,1)S(1)}, bf16[64,1024]{1,0:T(8,128)(2,1)S(1)}, u32[]{:S(2)}, u32[]{:S(2)}) collective-permute-start(bf16[64,1024]{1,0:T(8,128)(2,1)S(1)} %maximum_select_fusion.7), channel_id=1, source_target_pairs={{0,16},{8,24},{16,0},{24,8},{1,17},{9,25},{17,1},{25,9},{2,18},{10... | collective-permute-start | bytes 393224 | tf_op jit(solution)/shard_map/ppermute | solution.py:135
  147.9 4.2 %collective-permute-done.16 = bf16[64,1024]{1,0:T(8,128)(2,1)S(1)} collective-permute-done((bf16[64,1024]{1,0:T(8,128)(2,1)S(1)}, bf16[64,1024]{1,0:T(8,128)(2,1)S(1)}, u32[]{:S(2)}, u32[]{:S(2)}) %collective-permute-start.16) | collective-permute-done | bytes 131104 | tf_op jit(solution)/shard_map/ppermute | solution.py:135
  152.1 3.0 %collective-permute-start.17 = (bf16[128,1024]{1,0:T(8,128)(2,1)S(1)}, bf16[128,1024]{1,0:T(8,128)(2,1)S(1)}, u32[]{:S(2)}, u32[]{:S(2)}) collective-permute-start(bf16[128,1024]{1,0:T(8,128)(2,1)S(1)} %maximum_select_fusion.5), channel_id=1, source_target_pairs={{0,1},{1,0},{2,3},{3,2},{4,5},{5,4},{6,7},{7,6},{8,9},{9,8},{10,11... | collective-permute-start | bytes 786440 | tf_op jit(solution)/shard_map/ppermute | solution.py:135
  158.3 2.6 %collective-permute-start.9 = (bf16[512,1024]{1,0:T(8,128)(2,1)S(1)}, bf16[512,1024]{1,0:T(8,128)(2,1)S(1)}, u32[]{:S(2)}, u32[]{:S(2)}) collective-permute-start(bf16[512,1024]{1,0:T(8,128)(2,1)S(1)} %copy-done.7), channel_id=1, source_target_pairs={{1,0},{2,1},{3,2},{4,3},{5,4},{6,5},{7,6},{9,8},{10,9},{11,10},{12... | collective-permute-start | bytes 3145736 | tf_op jit(solution)/shard_map/ppermute | solution.py:197
  160.8 2.2 %collective-permute-start.5 = (bf16[512,1024]{1,0:T(8,128)(2,1)S(1)}, bf16[512,1024]{1,0:T(8,128)(2,1)S(1)}, u32[]{:S(2)}, u32[]{:S(2)}) collective-permute-start(bf16[512,1024]{1,0:T(8,128)(2,1)S(1)} %copy-done.5), channel_id=1, source_target_pairs={{1,0},{2,1},{3,2},{4,3},{5,4},{6,5},{7,6},{9,8},{10,9},{11,10},{12... | collective-permute-start | bytes 3145736 | tf_op jit(solution)/shard_map/ppermute | solution.py:197
  163.2 9.0 %collective-permute-done.18 = bf16[256,1024]{1,0:T(8,128)(2,1)S(1)} collective-permute-done((bf16[256,1024]{1,0:T(8,128)(2,1)S(1)}, bf16[256,1024]{1,0:T(8,128)(2,1)S(1)}, u32[]{:S(2)}, u32[]{:S(2)}) %collective-permute-start.18) | collective-permute-done | bytes 524320 | tf_op jit(solution)/shard_map/ppermute | solution.py:135
  172.6 2.0 collective-permute-start.19
  177.2 7.9 %collective-permute-done.9 = bf16[512,1024]{1,0:T(8,128)(2,1)S(1)} collective-permute-done((bf16[512,1024]{1,0:T(8,128)(2,1)S(1)}, bf16[512,1024]{1,0:T(8,128)(2,1)S(1)}, u32[]{:S(2)}, u32[]{:S(2)}) %collective-permute-start.9) | collective-permute-done | bytes 1048608 | tf_op jit(solution)/shard_map/ppermute | solution.py:197
  185.0 11.2 %collective-permute-done.5 = bf16[512,1024]{1,0:T(8,128)(2,1)S(1)} collective-permute-done((bf16[512,1024]{1,0:T(8,128)(2,1)S(1)}, bf16[512,1024]{1,0:T(8,128)(2,1)S(1)}, u32[]{:S(2)}, u32[]{:S(2)}) %collective-permute-start.5) | collective-permute-done | bytes 1048608 | tf_op jit(solution)/shard_map/ppermute | solution.py:197
  196.3 2.6 %fusion.3 = (bf16[1,512,1024]{2,1,0:T(8,128)(2,1)}, bf16[1,512,1024]{2,1,0:T(8,128)(2,1)}) fusion(f32[512,2048]{1,0:T(8,128)S(1)} %fusion.7, f32[512,1024]{1,0:T(8,128)S(1)} %copy-done.10, bf16[512,1024]{1,0:T(8,128)(2,1)S(1)} %collective-permute-done.9, f32[512,1024]{1,0:T(8,128)S(1)} %copy-done.9, bf16[512,1024]{1,0:T(8,128)(2,1)S(1)} %collective-permute-done.5), kind=kLoop, calls=%fused_computation.12 | loop fusion | flops 4194304 | bytes 12582912 | tf_op jit(solution)/shard_map/broadcast_in_dim | solution.py:203
  198.9 19.9 %collective-permute-done.19 = bf16[512,1024]{1,0:T(8,128)(2,1)S(1)} collective-permute-done((bf16[512,1024]{1,0:T(8,128)(2,1)S(1)}, bf16[512,1024]{1,0:T(8,128)(2,1)S(1)}, u32[]{:S(2)}, u32[]{:S(2)}) %collective-permute-start.19) | collective-permute-done | bytes 1048608 | tf_op jit(solution)/shard_map/ppermute | solution.py:135
  218.9 2.9 %convert_multiply_fusion = f32[1024,1024]{1,0:T(8,128)} fusion(bf16[512,1024]{1,0:T(8,128)(2,1)S(1)} %maximum_select_fusion.1, bf16[512,1024]{1,0:T(8,128)(2,1)S(1)} %collective-permute-done.19, pred[]{:T(512)S(6)} %ne.121), kind=kLoop, calls=%fused_computation.2 | loop fusion | flops 11534336 | bytes 6291457 | tf_op jit(solution)/shard_map/mul | solution.py:195
  (96 shorter events, 31.7 us)
Async XLA Ops:
  0.6 38.5 %collective-permute-start = (bf16[512,1024]{1,0:T(8,128)(2,1)}, bf16[512,1024]{1,0:T(8,128)(2,1)}, u32[]{:S(2)}, u32[]{:S(2)}) collective-permute-start(bf16[512,1024]{1,0:T(8,128)(2,1)} %bitcast.56), channel_id=1, source_target_pairs={{0,1},{1,2},{2,3},{3,4},{4,5},{5,6},{6,7},{8,9},{9,10},{10,11},{11... | collective-permute-start | bytes 3145736 | tf_op jit(solution)/shard_map/ppermute | solution.py:180
  4.5 34.7 %collective-permute-start.1 = (bf16[512,1024]{1,0:T(8,128)(2,1)}, bf16[512,1024]{1,0:T(8,128)(2,1)}, u32[]{:S(2)}, u32[]{:S(2)}) collective-permute-start(bf16[512,1024]{1,0:T(8,128)(2,1)} %bitcast.59), channel_id=1, source_target_pairs={{0,1},{1,2},{2,3},{3,4},{4,5},{5,6},{6,7},{8,9},{9,10},{10,11},{11... | collective-permute-start | bytes 3145736 | tf_op jit(solution)/shard_map/ppermute | solution.py:180
  11.1 6.9 %collective-permute-start.2 = (bf16[16,2048]{1,0:T(8,128)(2,1)S(1)}, bf16[16,2048]{1,0:T(8,128)(2,1)S(1)}, u32[]{:S(2)}, u32[]{:S(2)}) collective-permute-start(bf16[16,2048]{1,0:T(8,128)(2,1)S(1)} %constant_dynamic-update-slice_fusion), channel_id=1, source_target_pairs={{0,1},{1,0},{2,3},{3,2},{4,5},{5,4},{6,7},{7,6},{8,9},{9,8},{10,11... | collective-permute-start | bytes 196616 | tf_op jit(solution)/shard_map/ppermute | solution.py:135
  17.9 21.4 %copy-start.1 = (bf16[1,512,1024]{2,1,0:T(8,128)(2,1)S(1)}, bf16[1,512,1024]{2,1,0:T(8,128)(2,1)}, u32[]{:S(2)}) copy-start(bf16[1,512,1024]{2,1,0:T(8,128)(2,1)} %param.8) | copy-start | bytes 3145732
  18.0 13.5 %collective-permute-start.3 = (bf16[32,2048]{1,0:T(8,128)(2,1)S(1)}, bf16[32,2048]{1,0:T(8,128)(2,1)}, u32[]{:S(2)}, u32[]{:S(2)}) collective-permute-start(bf16[32,2048]{1,0:T(8,128)(2,1)S(1)} %maximum_select_fusion.6), channel_id=1, source_target_pairs={{0,2},{1,3},{2,0},{3,1},{4,6},{5,7},{6,4},{7,5},{8,10},{9,11},{10,... | collective-permute-start | bytes 393224 | tf_op jit(solution)/shard_map/ppermute | solution.py:135
  32.6 5.4 %collective-permute-start.4 = (bf16[64,2048]{1,0:T(8,128)(2,1)S(1)}, bf16[64,2048]{1,0:T(8,128)(2,1)}, u32[]{:S(2)}, u32[]{:S(2)}) collective-permute-start(bf16[64,2048]{1,0:T(8,128)(2,1)S(1)} %maximum_select_fusion.4), channel_id=1, source_target_pairs={{0,4},{1,5},{2,6},{3,7},{4,0},{5,1},{6,2},{7,3},{8,12},{9,13},{10,... | collective-permute-start | bytes 786440 | tf_op jit(solution)/shard_map/ppermute | solution.py:135
  39.3 52.0 %copy-start.11 = (bf16[1,512,1024]{2,1,0:T(8,128)(2,1)S(1)}, bf16[1,512,1024]{2,1,0:T(8,128)(2,1)}, u32[]{:S(2)}) copy-start(bf16[1,512,1024]{2,1,0:T(8,128)(2,1)} %param.11) | copy-start | bytes 3145732
  92.9 19.6 %collective-permute-start.10 = (bf16[512,1024]{1,0:T(8,128)(2,1)S(1)}, bf16[512,1024]{1,0:T(8,128)(2,1)S(1)}, u32[]{:S(2)}, u32[]{:S(2)}) collective-permute-start(bf16[512,1024]{1,0:T(8,128)(2,1)S(1)} %select_convert_fusion), channel_id=1, source_target_pairs={{0,4},{1,5},{2,6},{3,7},{4,0},{5,1},{6,2},{7,3},{8,12},{9,13},{10,... | collective-permute-start | bytes 3145736 | tf_op jit(solution)/shard_map/ppermute | solution.py:135
  113.3 11.5 %collective-permute-start.11 = (bf16[256,1024]{1,0:T(8,128)(2,1)S(1)}, bf16[256,1024]{1,0:T(8,128)(2,1)S(1)}, u32[]{:S(2)}, u32[]{:S(2)}) collective-permute-start(bf16[256,1024]{1,0:T(8,128)(2,1)S(1)} %select_convert_fusion.1), channel_id=1, source_target_pairs={{0,2},{1,3},{2,0},{3,1},{4,6},{5,7},{6,4},{7,5},{8,10},{9,11},{10,... | collective-permute-start | bytes 1572872 | tf_op jit(solution)/shard_map/ppermute | solution.py:135
  126.1 1.6 collective-permute-start.12
  129.0 8.7 %collective-permute-start.13 = (bf16[64,1024]{1,0:T(8,128)(2,1)S(1)}, bf16[64,1024]{1,0:T(8,128)(2,1)S(1)}, u32[]{:S(2)}, u32[]{:S(2)}) collective-permute-start(bf16[64,1024]{1,0:T(8,128)(2,1)S(1)} %select_convert_fusion.3), channel_id=1, source_target_pairs={{0,16},{8,24},{16,0},{24,8},{1,17},{9,25},{17,1},{25,9},{2,18},{10... | collective-permute-start | bytes 393224 | tf_op jit(solution)/shard_map/ppermute | solution.py:135
  137.8 3.3 %collective-permute-start.14 = (bf16[32,1024]{1,0:T(8,128)(2,1)S(1)}, bf16[32,1024]{1,0:T(8,128)(2,1)S(1)}, u32[]{:S(2)}, u32[]{:S(2)}) collective-permute-start(bf16[32,1024]{1,0:T(8,128)(2,1)S(1)} %select_convert_fusion.5), channel_id=1, source_target_pairs={{0,8},{8,0},{16,24},{24,16},{1,9},{9,1},{17,25},{25,17},{2,10},{10... | collective-permute-start | bytes 196616 | tf_op jit(solution)/shard_map/ppermute | solution.py:135
  138.8 22.0 %copy-start.5 = (bf16[512,1024]{1,0:T(8,128)(2,1)S(1)}, bf16[512,1024]{1,0:T(8,128)(2,1)}, u32[]{:S(2)}) copy-start(bf16[512,1024]{1,0:T(8,128)(2,1)} %copy-done.4) | copy-start | bytes 3145732
  138.8 9.0 %collective-permute-start.6 = (bf16[64,2048]{1,0:T(8,128)(2,1)S(1)}, bf16[64,2048]{1,0:T(8,128)(2,1)S(1)}, u32[]{:S(2)}, u32[]{:S(2)}) collective-permute-start(bf16[64,2048]{1,0:T(8,128)(2,1)S(1)} %broadcast_select_fusion), channel_id=1, source_target_pairs={{0,4},{1,5},{2,6},{3,7},{4,0},{5,1},{6,2},{7,3},{8,12},{9,13},{10,... | collective-permute-start | bytes 786440 | tf_op jit(solution)/shard_map/ppermute | solution.py:135
  141.1 3.5 %collective-permute-start.15 = (bf16[32,1024]{1,0:T(8,128)(2,1)S(1)}, bf16[32,1024]{1,0:T(8,128)(2,1)S(1)}, u32[]{:S(2)}, u32[]{:S(2)}) collective-permute-start(bf16[32,1024]{1,0:T(8,128)(2,1)S(1)} %add_convert_fusion), channel_id=1, source_target_pairs={{0,8},{8,0},{16,24},{24,16},{1,9},{9,1},{17,25},{25,17},{2,10},{10... | collective-permute-start | bytes 196616 | tf_op jit(solution)/shard_map/ppermute | solution.py:135
  144.6 7.4 %collective-permute-start.16 = (bf16[64,1024]{1,0:T(8,128)(2,1)S(1)}, bf16[64,1024]{1,0:T(8,128)(2,1)S(1)}, u32[]{:S(2)}, u32[]{:S(2)}) collective-permute-start(bf16[64,1024]{1,0:T(8,128)(2,1)S(1)} %maximum_select_fusion.7), channel_id=1, source_target_pairs={{0,16},{8,24},{16,0},{24,8},{1,17},{9,25},{17,1},{25,9},{2,18},{10... | collective-permute-start | bytes 393224 | tf_op jit(solution)/shard_map/ppermute | solution.py:135
  152.1 4.9 %collective-permute-start.17 = (bf16[128,1024]{1,0:T(8,128)(2,1)S(1)}, bf16[128,1024]{1,0:T(8,128)(2,1)S(1)}, u32[]{:S(2)}, u32[]{:S(2)}) collective-permute-start(bf16[128,1024]{1,0:T(8,128)(2,1)S(1)} %maximum_select_fusion.5), channel_id=1, source_target_pairs={{0,1},{1,0},{2,3},{3,2},{4,5},{5,4},{6,7},{7,6},{8,9},{9,8},{10,11... | collective-permute-start | bytes 786440 | tf_op jit(solution)/shard_map/ppermute | solution.py:135
  155.2 7.9 %collective-permute-start.7 = (bf16[32,2048]{1,0:T(8,128)(2,1)S(1)}, bf16[32,2048]{1,0:T(8,128)(2,1)S(1)}, u32[]{:S(2)}, u32[]{:S(2)}) collective-permute-start(bf16[32,2048]{1,0:T(8,128)(2,1)S(1)} %select_convert_fusion.4), channel_id=1, source_target_pairs={{0,2},{1,3},{2,0},{3,1},{4,6},{5,7},{6,4},{7,5},{8,10},{9,11},{10,... | collective-permute-start | bytes 393224 | tf_op jit(solution)/shard_map/ppermute | solution.py:135
  157.2 15.0 %collective-permute-start.18 = (bf16[256,1024]{1,0:T(8,128)(2,1)S(1)}, bf16[256,1024]{1,0:T(8,128)(2,1)S(1)}, u32[]{:S(2)}, u32[]{:S(2)}) collective-permute-start(bf16[256,1024]{1,0:T(8,128)(2,1)S(1)} %maximum_select_fusion.3), channel_id=1, source_target_pairs={{0,2},{1,3},{2,0},{3,1},{4,6},{5,7},{6,4},{7,5},{8,10},{9,11},{10,... | collective-permute-start | bytes 1572872 | tf_op jit(solution)/shard_map/ppermute | solution.py:135
  158.3 26.8 %collective-permute-start.9 = (bf16[512,1024]{1,0:T(8,128)(2,1)S(1)}, bf16[512,1024]{1,0:T(8,128)(2,1)S(1)}, u32[]{:S(2)}, u32[]{:S(2)}) collective-permute-start(bf16[512,1024]{1,0:T(8,128)(2,1)S(1)} %copy-done.7), channel_id=1, source_target_pairs={{1,0},{2,1},{3,2},{4,3},{5,4},{6,5},{7,6},{9,8},{10,9},{11,10},{12... | collective-permute-start | bytes 3145736 | tf_op jit(solution)/shard_map/ppermute | solution.py:197
  160.8 35.4 %collective-permute-start.5 = (bf16[512,1024]{1,0:T(8,128)(2,1)S(1)}, bf16[512,1024]{1,0:T(8,128)(2,1)S(1)}, u32[]{:S(2)}, u32[]{:S(2)}) collective-permute-start(bf16[512,1024]{1,0:T(8,128)(2,1)S(1)} %copy-done.5), channel_id=1, source_target_pairs={{1,0},{2,1},{3,2},{4,3},{5,4},{6,5},{7,6},{9,8},{10,9},{11,10},{12... | collective-permute-start | bytes 3145736 | tf_op jit(solution)/shard_map/ppermute | solution.py:197
  172.6 46.3 %collective-permute-start.19 = (bf16[512,1024]{1,0:T(8,128)(2,1)S(1)}, bf16[512,1024]{1,0:T(8,128)(2,1)S(1)}, u32[]{:S(2)}, u32[]{:S(2)}) collective-permute-start(bf16[512,1024]{1,0:T(8,128)(2,1)S(1)} %maximum_select_fusion.1), channel_id=1, source_target_pairs={{0,4},{1,5},{2,6},{3,7},{4,0},{5,1},{6,2},{7,3},{8,12},{9,13},{10,... | collective-permute-start | bytes 3145736 | tf_op jit(solution)/shard_map/ppermute | solution.py:135
  174.7 1.8 collective-permute-start.8
  175.7 20.6 %copy-start.10 = (f32[512,1024]{1,0:T(8,128)S(1)}, f32[512,1024]{1,0:T(8,128)}, u32[]{:S(2)}) copy-start(f32[512,1024]{1,0:T(8,128)} %get-tuple-element.17) | copy-start | bytes 6291460
  (10 other events, 88.1 us)
